TPU v7x, 32 devices: a whole 2x2x4 slice. The times are simulated.
32 devices in a mesh: wide: 8 (over y, x, core), narrow: 4 (over z).
Axes of the slice: x: 2, y: 2, z: 4, core: 2. Of those that a mesh axis runs over, the one named last changes fastest.
Arguments:
- latents: bfloat16 [2, 32, 16, 16, 768], P(None, ('wide', 'narrow')), may hold values from -6 to 6
- buckets: int32 [2, 32], P(None, ('wide', 'narrow')), may hold values from 0 to 2
- step_ids: int32 [2, 32], P(None, ('wide', 'narrow')), may hold values from 0 to 999
- qkv_spatial: bfloat16 [1769472], P(('wide', 'narrow')), may hold values from -0.21875 to 0.21875
- proj_spatial: bfloat16 [589824], P(('wide', 'narrow')), may hold values from -0.625 to 0.625
- qkv_temporal: bfloat16 [1769472], P(('wide', 'narrow')), may hold values from -0.21875 to 0.21875
- proj_temporal: bfloat16 [589824], P(('wide', 'narrow')), may hold values from -0.4375 to 0.4375
- up_weight: bfloat16 [2359296], P(('wide', 'narrow')), may hold values from -0.21875 to 0.21875
- down_weight: bfloat16 [2359296], P(('wide', 'narrow')), may hold values from -0.109375 to 0.109375
- ada_weight: bfloat16 [5308416], P(('wide', 'narrow')), may hold values from -0.21875 to 0.21875
- biases: bfloat16 [10752], P(('wide', 'narrow')), may hold values from -3 to 3
- cotangent: bfloat16 [2, 32, 16, 16, 768], P(None, ('wide', 'narrow')), may hold values from -6 to 6
Outputs:
- output: bfloat16 [2, 32, 16, 16, 768], P(None, ('wide', 'narrow'))
- latents_grad: float32 [2, 32, 16, 16, 768], P(None, ('wide', 'narrow'))
- qkv_spatial_grad: float32 [1769472], P(('wide', 'narrow'))
- proj_spatial_grad: float32 [589824], P(('wide', 'narrow'))
- qkv_temporal_grad: float32 [1769472], P(('wide', 'narrow'))
- proj_temporal_grad: float32 [589824], P(('wide', 'narrow'))
- up_weight_grad: float32 [2359296], P(('wide', 'narrow'))
- down_weight_grad: float32 [2359296], P(('wide', 'narrow'))
- ada_weight_grad: float32 [5308416], P(('wide', 'narrow'))
- biases_grad: float32 [10752], P(('wide', 'narrow'))
Inputs may be any that keep to these rules, and one draw needn't show every extreme that they name: `buckets`: an item's bucket sets how many leading spatial positions of each of its frames hold data: 16, 8 or 2 for 0, 1 or 2.
All inputs are finite; a program needn't handle non-finite values.
Results may differ from a plain program's by a relative error of at most 0.02.
Values may be sent and summed in bfloat16 or wider, within the bound.
A program may use at most 320 MiB of HBM per device.

v0:
```python
import math

import jax
import jax.numpy as jnp
from jax import lax
from jax.experimental import pallas as pl
from jax.experimental.pallas import tpu as pltpu
from jax.sharding import PartitionSpec as P

D = 768
HEADS = 12
HD = 64
FF = 3072
AXES = ("wide", "narrow")
EPS = 1e-06
MASKED = -1e30
F32 = jnp.float32
BF16 = jnp.bfloat16
GELU = math.sqrt(2.0 / math.pi)
MESH = pl.DeviceIdType.MESH
DEVICES = 32
OWNERS = 9 * D // 256
SHARE = (10 * D + FF) // DEVICES
SPATIAL = 16
TOKENS = 256
VMEM_LIMIT = 67_000_000


def dot(a, b):
    return jnp.dot(a, b, preferred_element_type=F32)


def place():
    w, z = lax.axis_index("wide"), lax.axis_index("narrow")
    return w // 4, (w // 2) % 2, w % 2, z


def device_at(y, x, c, z):
    return {"wide": (y * 2 + x) * 2 + c, "narrow": z}


def remote(src, dst, send, recv, target):
    return pltpu.make_async_remote_copy(
        src_ref=src, dst_ref=dst, send_sem=send, recv_sem=recv,
        device_id=target, device_id_type=MESH,
    )


class Sender:
    def __init__(self):
        self.copies = []

    def go(self, src, dst, send, recv, target):
        copy = remote(src, dst, send, recv, target)
        copy.start()
        self.copies.append(copy)

    def drain(self):
        for copy in self.copies:
            copy.wait_send()


def timestep_condition(step_values):
    half_width = D // 2
    frequency = jnp.exp(-math.log(10000.0) * jnp.arange(half_width, dtype=F32) / half_width)
    angles = step_values.astype(F32)[:, None] * frequency
    return jax.nn.silu(jnp.concatenate([jnp.cos(angles), jnp.sin(angles)], axis=-1)).astype(BF16)


class Gather:
    SEMAPHORES = (3, 3, 10, 10, 3, 3, 3, 3)

    def __init__(self, here, sender, own, out, semaphores, local):
        self.here, self.sender, self.own, self.out, self.local = here, sender, own, out, local
        self.zs, self.zr, self.cs, self.cr, self.xs, self.xr, self.ys, self.yr = semaphores
        y, x, c, z = here
        self.sib = device_at(y, x, 1 - c, z)
        self.xn = device_at(y, 1 - x, c, z)
        self.yn = device_at(1 - y, x, c, z)

    @staticmethod
    def scratch(count):
        kinds = [pltpu.SemaphoreType.DMA((count, k)) for k in Gather.SEMAPHORES]
        return kinds + [pltpu.SemaphoreType.DMA((count,))]

    def start(self, i):
        y, x, c, z = self.here
        mine = self.out[i].at[y, x, c, z]
        for step in (2, 1, 3):
            self.sender.go(
                self.own[i], mine, self.zs.at[i, step - 1],
                self.zr.at[i, step - 1], device_at(y, x, c, (z + step) % 4),
            )
        pltpu.make_async_copy(self.own[i], mine, self.local.at[i]).start()
        self.sender.go(self.own[i], mine, self.cs.at[i, 0], self.cr.at[i, 0], self.sib)

    def along(self, ref, send, recv, target):
        self.sender.go(ref, ref, send, recv, target)

    def arrived(self, ref, send, recv):
        remote(ref, ref, send, recv, self.sib).wait_recv()

    def across(self, i, k, ref):
        self.sender.go(ref, ref, self.cs.at[i, k], self.cr.at[i, k], self.sib)

    def stage1(self, i):
        y, x, c, z = self.here
        out = self.out[i]
        pltpu.make_async_copy(self.own[i], out.at[y, x, c, z], self.local.at[i]).wait()
        for step in (1, 2, 3):
            self.arrived(out.at[y, x, c, (z + 4 - step) % 4], self.zs.at[i, step - 1], self.zr.at[i, step - 1])
        low, high = out.at[y, x, c, pl.ds(0, 2)], out.at[y, x, c, pl.ds(2, 2)]
        self.along(low, self.xs.at[i, 0], self.xr.at[i, 0], self.xn)
        self.along(high, self.ys.at[i, 0], self.yr.at[i, 0], self.yn)
        self.along(high, self.xs.at[i, 1], self.xr.at[i, 1], self.xn)
        self.along(low, self.ys.at[i, 1], self.yr.at[i, 1], self.yn)
        for step in (1, 2, 3):
            self.across(i, step, out.at[y, x, c, (z + 4 - step) % 4])

    def stage2(self, i):
        y, x, c, z = self.here
        low_x = self.out[i].at[y, 1 - x, c, pl.ds(0, 2)]
        high_y = self.out[i].at[1 - y, x, c, pl.ds(2, 2)]
        self.arrived(low_x, self.xs.at[i, 0], self.xr.at[i, 0])
        self.along(low_x, self.ys.at[i, 2], self.yr.at[i, 2], self.yn)
        self.arrived(high_y, self.ys.at[i, 0], self.yr.at[i, 0])
        self.along(high_y, self.xs.at[i, 2], self.xr.at[i, 2], self.xn)
        self.across(i, 4, low_x)
        self.across(i, 5, high_y)

    def stage3(self, i):
        y, x, c, z = self.here
        out = self.out[i]
        arrivals = (
            (out.at[y, 1 - x, c, pl.ds(2, 2)], self.xs.at[i, 1], self.xr.at[i, 1]),
            (out.at[1 - y, x, c, pl.ds(0, 2)], self.ys.at[i, 1], self.yr.at[i, 1]),
            (out.at[1 - y, 1 - x, c, pl.ds(2, 2)], self.xs.at[i, 2], self.xr.at[i, 2]),
            (out.at[1 - y, 1 - x, c, pl.ds(0, 2)], self.ys.at[i, 2], self.yr.at[i, 2]),
        )
        for k, (ref, send, recv) in enumerate(arrivals):
            self.arrived(ref, send, recv)
            self.across(i, 6 + k, ref)

    def finish(self, i):
        y, x, c, z = self.here
        o = 1 - c
        out = self.out[i]
        arrivals = [out.at[y, x, o, (z + 4 - step) % 4] for step in (0, 1, 2, 3)]
        arrivals += [
            out.at[y, 1 - x, o, pl.ds(0, 2)],
            out.at[1 - y, x, o, pl.ds(2, 2)],
            out.at[y, 1 - x, o, pl.ds(2, 2)],
            out.at[1 - y, x, o, pl.ds(0, 2)],
            out.at[1 - y, 1 - x, o, pl.ds(2, 2)],
            out.at[1 - y, 1 - x, o, pl.ds(0, 2)],
        ]
        for k, ref in enumerate(arrivals):
            self.arrived(ref, self.cs.at[i, k], self.cr.at[i, k])


class Spread:
    SEMAPHORES = (3, 3, 6, 6, 6, 6, 2, 2, 16, 16)

    def __init__(self, here, own, out, semaphores, local, pairs):
        self.here, self.own, self.out, self.local = here, own, out, local
        self.pairs = pairs
        self.zs, self.zr, self.xs, self.xr, self.ys, self.yr, self.ps, self.pr, self.cs, self.cr = semaphores
        self.sent = []
        y, x, c, z = here
        self.sib = device_at(y, x, 1 - c, z)
        self.xn = device_at(y, 1 - x, c, z)
        self.yn = device_at(1 - y, x, c, z)
        self.partner = z + 1 - 2 * (z % 2)
        self.opposite = (z + 2) % 4
        self.zp = device_at(y, x, c, self.partner)

    @staticmethod
    def scratch(count):
        kinds = [pltpu.SemaphoreType.DMA((count, k)) for k in Spread.SEMAPHORES]
        return kinds + [pltpu.SemaphoreType.DMA((count,))]

    def go(self, i, k, src, dst, send, recv, target):
        remote(src, dst, send.at[i, k], recv.at[i, k], target).start()
        self.sent.append((i, k, send, recv))

    def drain(self):
        for i, k, send, recv in self.sent:
            remote(self.own[i], self.own[i], send.at[i, k], recv.at[i, k], self.sib).wait_send()

    def to_x(self, i, k, ref):
        self.go(i, k, ref, ref, self.xs, self.xr, self.xn)

    def to_y(self, i, k, ref):
        self.go(i, k, ref, ref, self.ys, self.yr, self.yn)

    def across(self, i, k, ref):
        self.go(i, k, ref, ref, self.cs, self.cr, self.sib)

    def arrived(self, ref, send, recv):
        remote(ref, ref, send, recv, self.sib).wait_recv()

    def from_z(self, step):
        return (self.here[3] + 4 - step) % 4

    def beside(self, i):
        y, x, c, z = self.here
        own, mine = self.own[i], self.out[i].at[y, x, c, z]
        pltpu.make_async_copy(own, mine, self.local.at[i]).start()
        self.go(i, 0, own, mine, self.xs, self.xr, self.xn)
        self.go(i, 0, own, mine, self.ys, self.yr, self.yn)
        self.go(i, 0, own, mine, self.cs, self.cr, self.sib)

    def along(self, i):
        y, x, c, z = self.here
        own, mine = self.own[i], self.out[i].at[y, x, c, z]
        for step in (2, 1, 3):
            there = device_at(y, x, c, (z + step) % 4)
            self.go(i, step - 1, own, mine, self.zs, self.zr, there)

    def column(self, i):
        y, x, c, z = self.here
        for step in (2, 1, 3):
            ref = self.out[i].at[y, x, c, self.from_z(step)]
            self.arrived(ref, self.zs.at[i, step - 1], self.zr.at[i, step - 1])
            self.to_x(i, step, ref)
            self.to_y(i, step, ref)
            self.across(i, step, ref)

    def sides(self, i):
        y, x, c, z = self.here
        for step in (0, 2, 1, 3):
            from_x = self.out[i].at[y, 1 - x, c, self.from_z(step)]
            self.arrived(from_x, self.xs.at[i, step], self.xr.at[i, step])
            if step == 0 or step == 2 and not self.pairs[i]:
                self.to_y(i, 4 + step // 2, from_x)
            self.across(i, 4 + step, from_x)
            from_y = self.out[i].at[1 - y, x, c, self.from_z(step)]
            self.arrived(from_y, self.ys.at[i, step], self.yr.at[i, step])
            if step == 2 and self.pairs[i]:
                self.to_x(i, 4, from_y)
            if step % 2 and not self.pairs[i]:
                self.to_x(i, 4 + step // 2, from_y)
            self.across(i, 8 + step, from_y)

    def diagonal(self, i):
        y, x, c, z = self.here
        where = self.out[i].at[1 - y, 1 - x, c]
        blocks = self.corner(i)
        if self.pairs[i]:
            lanes = ((self.ys, self.yr, 4), (self.xs, self.xr, 4))
        else:
            lanes = ((self.ys, self.yr, 4), (self.ys, self.yr, 5), (self.xs, self.xr, 4), (self.xs, self.xr, 5))
        for k, (send, recv, n) in enumerate(lanes):
            ref = where.at[blocks[k]]
            self.arrived(ref, send.at[i, n], recv.at[i, n])
            if self.pairs[i]:
                self.go(i, k, ref, ref, self.ps, self.pr, self.zp)
            self.across(i, 12 + k, ref)

    def corner(self, i):
        if self.pairs[i]:
            return self.here[3], self.opposite, self.partner, (self.partner + 2) % 4
        return self.from_z(0), self.from_z(2), self.from_z(1), self.from_z(3)

    def pair(self, i):
        y, x, c, z = self.here
        where = self.out[i].at[1 - y, 1 - x, c]
        for k, block in enumerate(self.corner(i)[2:] if self.pairs[i] else ()):
            ref = where.at[block]
            self.arrived(ref, self.ps.at[i, k], self.pr.at[i, k])
            self.across(i, 14 + k, ref)

    def finish(self, i):
        y, x, c, z = self.here
        out, o = self.out[i], 1 - c
        pltpu.make_async_copy(self.own[i], out.at[y, x, c, z], self.local.at[i]).wait()
        arrivals = [out.at[y, x, o, self.from_z(step)] for step in range(4)]
        arrivals += [out.at[y, 1 - x, o, self.from_z(step)] for step in range(4)]
        arrivals += [out.at[1 - y, x, o, self.from_z(step)] for step in range(4)]
        arrivals += [out.at[1 - y, 1 - x, o, block] for block in self.corner(i)]
        for k, ref in enumerate(arrivals):
            self.arrived(ref, self.cs.at[i, k], self.cr.at[i, k])


PAIRED = (True, True, False, True, True, True, False, False)
SPREAD_STEPS = (
    (("A", 0), ("B", 0), ("A", 6),), (), (), (), (("A", 2),), (), (("A", 4), ("A", 7),), (), (),
    (("A", 1), ("B", 1), ("A", 3),), (), (("C", 0),), (("B", 2),), (), (("B", 4),), (("B", 3), ("C", 1),), (), (),
    (("X", 0), ("X", 1), ("C", 2), ("D", 0), ("D", 1), ("C", 4), ("P", 0),),
    (("B", 5), ("B", 6), ("P", 1), ("X", 2), ("C", 3),), (), (), (("B", 7), ("X", 4),), (),
    (("D", 2), ("A", 5), ("C", 5),), (("X", 3),), (), (("D", 4),), (), (("C", 6),), (), (),
    (("X", 5), ("P", 4), ("D", 3),), (("C", 7),), (("P", 3),), (("D", 5), ("X", 6),), (), (), (),
    (("P", 5), ("X", 7),), (), (), (("D", 6),), (("D", 7),), (), (),
)


class Steps:
    def __init__(self, calls, table):
        self.calls, self.table = calls, list(table)

    def run(self, steps):
        for kind, i in steps:
            self.calls[kind](i)

    def __call__(self):
        self.run(self.table.pop(0))

    def rolled(self, count, *parts):
        due = [[self.table.pop(0) if k % every == every - 1 else () for _, _, every in parts] for k in range(count)]

        def turn(j, _):
            for n, (body, also, _) in enumerate(parts):
                body(j)
                for k in range(count):
                    if k in also or due[k][n]:
                        @pl.when(j == k)
                        def _(k=k, n=n, also=also):
                            if k in also:
                                also[k]()
                            self.run(due[k][n])

            return 0

        lax.fori_loop(0, count, turn, 0)


class Names:
    def __init__(self, names, refs):
        for name, ref in zip(names, refs, strict=True):
            setattr(self, name, ref)


def rows_of(item, step, size):
    return pl.ds(pl.multiple_of(item * TOKENS + step * size, size), size)


def lane_cols(start, size=128):
    return pl.ds(start if isinstance(start, int) else pl.multiple_of(start, 128), size)


def dot_t(a, b):
    return lax.dot_general(a, b, (((1,), (1,)), ((), ())), preferred_element_type=F32)


def t_dot(a, b):
    return lax.dot_general(a, b, (((0,), (0,)), ((), ())), preferred_element_type=F32)


def weight_block(ref, start, size):
    cols = ref[:, :, :, :, :, lane_cols(start, size)]
    return cols.reshape(-1, size)


def two_heads(x, scale):
    lane = lax.broadcasted_iota(jnp.int32, x.shape, 1)
    x = x * jnp.asarray(scale, x.dtype)
    zero = jnp.zeros_like(x)
    return jnp.concatenate([jnp.where(lane < HD, x, zero), jnp.where(lane >= HD, x, zero)], axis=0)


def pick_heads(first, second):
    lane = lax.broadcasted_iota(jnp.int32, first.shape, 1)
    return jnp.where(lane < HD, first, second)


def norm_rows(v):
    centre = v - jnp.mean(v, axis=-1, keepdims=True)
    inverse = lax.rsqrt(jnp.mean(centre * centre, axis=-1, keepdims=True) + EPS)
    return centre * inverse, inverse


CHUNK = 32
PAIRS = HEADS // 2
TENSORS = ("qs", "ps", "qt", "pt", "up", "down")
PIECES = (("qs", 0, 3 * D), ("ps", 0, D), ("qt", 0, 3 * D), ("pt", 0, D))
PIECES += tuple((t, k * n, n) for t, n in (("up", FF // 2), ("down", D // 2)) for k in range(2))


def save_shapes(tokens):
    rows = 2 * tokens
    attention = {
        "n": ((rows, D), BF16), "r": ((rows, 1), F32), "h": ((rows, D), BF16),
        "q": ((rows, 3 * D), BF16), "p": ((rows, 2 * PAIRS * tokens), BF16),
        "c": ((rows, D), BF16), "a": ((rows, D), BF16),
    }
    out = {}
    for k in (1, 2):
        out.update({name + str(k): spec for name, spec in attention.items()})
    out.update({
        "n3": ((rows, D), BF16), "r3": ((rows, 1), F32), "h3": ((rows, D), BF16),
        "g": ((rows, FF), BF16), "gp": ((rows, FF), BF16), "mods": ((9, 8, D), F32),
    })
    return out


def unflatten(s, flat, own):
    rows, size = own.shape
    stride = size // 128
    s.stage[pl.ds(0, flat.shape[0]), :] = flat[...].astype(F32)
    for k in range(stride):
        own[:, k * 128 : (k + 1) * 128] = s.stage[pl.ds(k, rows, stride=stride), :].astype(BF16)


def lengths(buckets):
    return jnp.where(buckets == 0, SPATIAL, jnp.where(buckets == 1, SPATIAL // 2, SPATIAL // 8))


def valid_rows(s):
    length = lengths(s.buckets[...])
    spot = lax.broadcasted_iota(jnp.int32, (TOKENS, 1), 0) % SPATIAL
    for item in range(2):
        s.valid[item * TOKENS : (item + 1) * TOKENS, :] = (spot < length[item : item + 1, :]).astype(F32)


def norm_into(s, k, shift, scale, rows, item, v):
    n, r = norm_rows(v)
    getattr(s, "n" + k)[rows, :] = n.astype(BF16)
    getattr(s, "r" + k)[rows, :] = r
    h = n * (1.0 + s.mods[scale, item : item + 1, :]) + s.mods[shift, item : item + 1, :]
    getattr(s, "h" + k)[rows, :] = h.astype(BF16)


def project(s, k, weight, point):
    h, q = getattr(s, "h" + k), getattr(s, "q" + k)

    def column(j):
        q[:, lane_cols(j * D, D)] = dot(h[...], weight_block(weight, j * D, D)).astype(BF16)

    point.rolled(3, (column, {}, 1))


def attend(s, k, bias_of, first):
    q, p, c = getattr(s, "q" + k), getattr(s, "p" + k), getattr(s, "c" + k)

    def body(t, _):
        step = first + t
        item, pair = step // PAIRS, step % PAIRS
        rows = pl.ds(pl.multiple_of(item * TOKENS, TOKENS), TOKENS)
        at = [lane_cols(pair * 128 + j * D) for j in range(3)]
        scores = dot_t(two_heads(q[rows, at[0]], HD ** (-0.5)), q[rows, at[1]])
        scores = (scores.reshape(2, TOKENS, TOKENS) + bias_of(item)).reshape(2 * TOKENS, TOKENS)
        expanded = jnp.exp(scores - jnp.max(scores, axis=-1, keepdims=True))
        soft = (expanded * (1.0 / jnp.sum(expanded, axis=-1, keepdims=True))).astype(BF16)
        p[:, lane_cols(step * TOKENS, TOKENS)] = soft
        context = dot(soft, q[rows, at[2]])
        c[rows, at[0]] = pick_heads(context[:TOKENS], context[TOKENS:]).astype(BF16)
        return 0

    lax.fori_loop(0, PAIRS // 2, body, 0)


def after_attention(s, k, next_k, weight, gate, shift, scale):
    s.acc[...] = dot(getattr(s, "c" + k)[...], weight_block(weight, 0, D))
    for item in range(2):
        def body(t, _):
            rows = rows_of(item, t, CHUNK)
            a = s.acc[rows, :]
            v = s.x[rows, :] + s.mods[gate, item : item + 1, :] * a
            s.x[rows, :] = v
            getattr(s, "a" + k)[rows, :] = a.astype(BF16)
            norm_into(s, next_k, shift, scale, rows, item, v)
            return 0

        lax.fori_loop(0, TOKENS // CHUNK, body, 0)


def flat_bias(s):
    s.bias[...] = jnp.zeros_like(s.bias)
    for d in range(DEVICES):
        y, x, c, z = d // 16, (d // 8) % 2, (d // 4) % 2, d % 4
        piece = s.small_all[y, x, c, z].astype(F32)[2:3, :512]
        lane = lax.broadcasted_iota(jnp.int32, piece.shape, 1)
        piece = jnp.where(lane < SHARE, piece, 0.0)
        start = d * SHARE
        if start % 128:
            piece = pltpu.roll(piece, start % 128, 1)
        low = start // 128 * 128
        s.bias[:, low : low + 512] = s.bias[:, low : low + 512] + piece


def forward_kernel(names, *refs):
    s = Names(names, refs)
    here = place()
    y, x, c, z = here
    me = ((y * 2 + x) * 2 + c) * 4 + z
    sender = Sender()
    weights = [getattr(s, "w_" + t).at[:, :, :, :, :, pl.ds(at, size)] for t, at, size in PIECES]
    own = [getattr(s, "own_" + t).at[:, pl.ds(at, size)] for t, at, size in PIECES]
    gather = Spread(here, own, weights, [getattr(s, f"gs{i}") for i in range(10)], s.gs10, PAIRED)
    calls = {"A": gather.beside, "B": gather.along, "C": gather.column}
    calls |= {"X": gather.sides, "D": gather.diagonal, "P": gather.pair}
    point = Steps(calls, SPREAD_STEPS)
    little = Gather(here, sender, [s.small], [s.small_all], [getattr(s, f"ls{i}") for i in range(8)], s.ls8)
    saves = []

    def save(*names):
        for name in names:
            copy = pltpu.make_async_copy(getattr(s, name), getattr(s, "out_" + name), s.save_sem.at[len(saves)])
            copy.start()
            saves.append(copy)

    def target(k):
        d = (me + k) % DEVICES
        return d, {"wide": d // 4, "narrow": d % 4}

    barrier = pltpu.get_barrier_semaphore()

    def signal(k, _):
        pl.semaphore_signal(barrier, inc=1, device_id=target(k)[1], device_id_type=MESH)
        return 0

    lax.fori_loop(1, DEVICES, signal, 0)
    s.little[...] = jnp.zeros_like(s.little)
    s.little[0:2, :] = s.conditions[...].astype(F32)
    s.little[2:3, :SHARE] = s.biases[...].astype(F32)
    s.small[...] = s.little[...].astype(BF16)
    unflatten(s, s.flat_ada, s.ada)
    pl.semaphore_wait(barrier, DEVICES - 1)

    def columns_copy(k):
        d, there = target(k)
        src = s.ada.at[:, lane_cols(d * 256, 256)]
        return d, remote(src, s.ada_cols.at[me], s.a_send.at[k], s.a_recv.at[me], there)

    little.start(0)

    def send_columns(k, _):
        d, copy = columns_copy(k)

        @pl.when(d < OWNERS)
        def _():
            copy.start()

        return 0

    lax.fori_loop(1, DEVICES, send_columns, 0)
    owner = me < OWNERS
    mine = jnp.minimum(me, OWNERS - 1)
    own_columns = pltpu.make_async_copy(s.ada.at[:, lane_cols(mine * 256, 256)], s.ada_cols.at[me], s.own_sem.at[0])
    own_columns.start()
    for t in TENSORS:
        unflatten(s, getattr(s, "flat_" + t), getattr(s, "own_" + t))
    point()

    place_of = lambda n: lax.broadcasted_iota(jnp.int32, (TOKENS, TOKENS), n)
    same_frame = place_of(0) // SPATIAL == place_of(1) // SPATIAL
    same_place = place_of(0) % SPATIAL == place_of(1) % SPATIAL
    for item in range(2):
        seen = lax.broadcasted_iota(jnp.int32, (1, TOKENS), 1) % SPATIAL < lengths(s.buckets[...])[item : item + 1, :]
        s.space_bias[item] = jnp.where(same_frame, jnp.where(seen, 0.0, MASKED), MASKED)
    s.time_bias[...] = jnp.where(same_place, 0.0, MASKED)
    valid_rows(s)
    point()
    point()
    little.stage1(0)
    point()
    little.stage2(0)
    point()
    little.stage3(0)
    point()
    little.finish(0)
    point()
    own_columns.wait()

    def modulation_copy(k):
        d, there = target(k)
        src = s.mod_cols.at[pl.ds(pl.multiple_of(d * 8, 8), 8)]
        return remote(src, s.mod_all.at[me], s.m_send.at[k], s.m_recv.at[me], there)

    own_mod = pltpu.make_async_copy(
        s.mod_cols.at[pl.ds(pl.multiple_of(me * 8, 8), 8)], s.mod_all.at[mine], s.own_sem.at[1]
    )

    conditions = s.small_all[...].reshape(DEVICES * 8, D)
    point()

    @pl.when(owner)
    def _():
        def wait_columns(k, _):
            d, there = target(k)
            remote(s.ada_cols.at[d], s.ada_cols.at[d], s.a_send.at[k], s.a_recv.at[d], there).wait_recv()
            return 0

        lax.fori_loop(1, DEVICES, wait_columns, 0)
        s.mod_cols[...] = dot(conditions, s.ada_cols[...].reshape(D, 256))

        def send_modulation(k, _):
            modulation_copy(k).start()
            return 0

        lax.fori_loop(1, DEVICES, send_modulation, 0)
        own_mod.start()

    point()
    flat_bias(s)
    point()
    part = D // DEVICES
    spot = lambda shape, n: lax.broadcasted_iota(jnp.int32, shape, n)
    col = spot((D, 128), 1)
    wanted = (spot((D, 128), 0) == me * part + col) & (col < part)
    mine_only = dot(conditions, wanted.astype(F32).astype(BF16)).astype(BF16)
    row, item = spot((D, DEVICES * 8), 0), spot((D, DEVICES * 8), 1)
    slot = row % part
    copy_of = (row // part == item // 8) & (slot // 9 == item % 8) & (slot < 18)
    s.chosen[...] = dot(copy_of.astype(F32).astype(BF16), mine_only).astype(BF16)
    for _ in range(6):
        point()

    @pl.when(owner)
    def _():
        own_mod.wait()

    def wait_modulation(k, _):
        d, there = target(k)

        @pl.when(d < OWNERS)
        def _():
            remote(s.mod_all.at[d], s.mod_all.at[d], s.m_send.at[k], s.m_recv.at[d], there).wait_recv()

        return 0

    lax.fori_loop(1, DEVICES, wait_modulation, 0)
    for j in range(9):
        row = jnp.concatenate([s.mod_all[3 * j + i] for i in range(3)], axis=1)
        s.mods[j] = row + s.bias[:, j * D : (j + 1) * D]
    save("mods")

    for item in range(2):
        def first(t, _):
            rows = rows_of(item, t, CHUNK)
            v = s.latents[rows, :].astype(F32)
            s.x[rows, :] = v
            norm_into(s, "1", 0, 1, rows, item, v)
            return 0

        lax.fori_loop(0, TOKENS // CHUNK, first, 0)
        point()
    save("n1", "r1", "h1")

    def ready(i):
        point()
        gather.finish(i)
        t, at, size = PIECES[i]
        if at + size == getattr(s, "w_" + t).shape[-1]:
            save("w_" + t)

    ready(0)
    project(s, "1", s.w_qs, point)
    space = lambda item: s.space_bias[item]
    point.rolled(4, (lambda k: attend(s, "1", space, 3 * k), {}, 1))
    ready(1)
    after_attention(s, "1", "2", s.w_ps, 2, 3, 4)
    save("q1", "p1", "c1", "a1", "n2", "r2", "h2")
    point()
    ready(2)
    project(s, "2", s.w_qt, point)
    time = lambda item: s.time_bias[...]
    point.rolled(4, (lambda k: attend(s, "2", time, 3 * k), {}, 1))
    ready(3)
    after_attention(s, "2", "3", s.w_pt, 5, 6, 7)
    save("q2", "p2", "c2", "a2", "n3", "r3", "h3")
    point()
    ready(4)

    def up(j):
        cols = lane_cols(j * D, D)
        s.acc[...] = dot(s.h3[...], weight_block(s.w_up, j * D, D))
        b_up = s.bias[:, lane_cols((9 + j) * D, D)]

        def activate(t, _):
            rows = rows_of(0, t, CHUNK)
            u = s.acc[rows, :] + b_up
            square = u * u
            th = jnp.tanh(u * (GELU + (GELU * 0.044715) * square))
            half = 0.5 * u
            s.g[rows, cols] = (half + half * th).astype(BF16)
            slope = 0.5 + 0.5 * th + half * (1.0 - th * th) * (GELU + (3 * GELU * 0.044715) * square)
            s.gp[rows, cols] = slope.astype(BF16)
            return 0

        lax.fori_loop(0, 2 * TOKENS // CHUNK, activate, 0)

    point.rolled(2, (up, {}, 1))
    ready(5)
    point.rolled(2, (lambda j: up(2 + j), {}, 1))
    save("g", "gp")
    s.acc[...] = jnp.zeros_like(s.acc)
    for half in range(2):
        ready(6 + half)
        cols = slice(half * D // 2, (half + 1) * D // 2)

        def down(j, _):
            w = s.w_down[j // 2, j % 2, :, :, :, cols].reshape(D, D // 2)
            s.acc[:, cols] = s.acc[:, cols] + dot(s.g[:, lane_cols(j * D, D)], w)
            return 0

        lax.fori_loop(0, FF // D, down, 0)
    b_down = s.bias[:, (9 + FF // D) * D : (10 + FF // D) * D]
    for item in range(2):
        gate = s.mods[8, item : item + 1, :]

        def last(t, total):
            rows = rows_of(item, t, CHUNK)
            m = s.acc[rows, :] + b_down
            valid = s.valid[rows, :]
            s.output[rows, :] = ((s.x[rows, :] + gate * m) * valid).astype(BF16)
            d3 = s.cotangent[rows, :].astype(F32) * valid
            return total + jnp.sum((d3 * m).reshape(CHUNK // 8, 8, D), axis=0)

        total = lax.fori_loop(0, TOKENS // CHUNK, last, jnp.zeros((8, D), F32))
        s.dga3[item : item + 1, :] = jnp.sum(total, axis=0, keepdims=True)

    def drain(k, _):
        d, copy = columns_copy(k)

        @pl.when(d < OWNERS)
        def _():
            copy.wait_send()

        @pl.when(owner)
        def _():
            modulation_copy(k).wait_send()

        return 0

    lax.fori_loop(1, DEVICES, drain, 0)
    sender.drain()
    gather.drain()
    for copy in saves:
        copy.wait()


def run_forward(conditions, biases, buckets, ada, shards, latents, cotangent):
    vmem, any_space = pl.BlockSpec(memory_space=pltpu.VMEM), pl.BlockSpec(memory_space=pl.ANY)
    saved = save_shapes(TOKENS)
    part = D // DEVICES
    own = {t: (4 * part, D) if t == "down" else (part, WIDTHS[t]) for t in TENSORS}
    weights = {"w_" + t: ((2, 2, 2, 4) + own[t], BF16) for t in TENSORS}
    kept = {**saved, **weights}
    rows = 2 * TOKENS
    ins = ["conditions", "biases", "buckets", "flat_ada"] + ["flat_" + t for t in TENSORS] + ["latents", "cotangent"]
    outs = ["output", "dga3", "chosen"] + ["out_" + name for name in kept]
    dma = pltpu.SemaphoreType.DMA
    scratch = {name: pltpu.VMEM(*spec) for name, spec in kept.items()}
    scratch |= {"own_" + t: pltpu.VMEM(shape, BF16) for t, shape in own.items()}
    scratch |= {
        "small": pltpu.VMEM((8, D), BF16), "little": pltpu.VMEM((8, D), F32),
        "stage": pltpu.VMEM(ada.shape, F32), "ada": pltpu.VMEM((part, 9 * D), BF16),
        "valid": pltpu.VMEM((rows, 1), F32),
        "small_all": pltpu.VMEM((2, 2, 2, 4, 8, D), BF16),
        "ada_cols": pltpu.VMEM((DEVICES, part, 256), BF16),
        "mod_cols": pltpu.VMEM((DEVICES * 8, 256), F32),
        "mod_all": pltpu.VMEM((OWNERS, 8, 256), F32),
        "bias": pltpu.VMEM((1, DEVICES * SHARE + 512), F32),
        "x": pltpu.VMEM((rows, D), F32),
        "acc": pltpu.VMEM((rows, D), F32),
        "space_bias": pltpu.VMEM((2, TOKENS, TOKENS), F32),
        "time_bias": pltpu.VMEM((TOKENS, TOKENS), F32),
        "save_sem": dma((len(kept),)),
        "a_send": dma((DEVICES,)), "a_recv": dma((DEVICES,)),
        "m_send": dma((DEVICES,)), "m_recv": dma((DEVICES,)), "own_sem": dma((2,)),
    }
    scratch |= {f"gs{i}": kind for i, kind in enumerate(Spread.scratch(len(PIECES)))}
    scratch |= {f"ls{i}": kind for i, kind in enumerate(Gather.scratch(1))}
    names = ins + outs + list(scratch)
    results = pl.pallas_call(
        lambda *refs: forward_kernel(names, *refs),
        out_shape=(jax.ShapeDtypeStruct((rows, D), BF16), jax.ShapeDtypeStruct((2, D), F32), jax.ShapeDtypeStruct((D, 128), BF16))
        + tuple(jax.ShapeDtypeStruct(*spec) for spec in kept.values()),
        in_specs=[vmem] * len(ins),
        out_specs=(vmem,) * 3 + (any_space,) * len(kept),
        scratch_shapes=list(scratch.values()),
        compiler_params=pltpu.CompilerParams(
            collective_id=1, has_side_effects=True, vmem_limit_bytes=VMEM_LIMIT
        ),
        name="forward",
    )(conditions, biases, buckets, ada, *shards, latents, cotangent)
    return results[0], results[1], results[2], dict(zip(kept, results[3:]))


class Scatter:
    SEMAPHORES = ((), (), (2,), (2,), (4,), (4,), (4,), (4,), (4,), (4,), (3,), (3,))
    LEADING = ((2, 2, 4), (2,), (4,), (4,), (4,), (3,))

    def __init__(self, here, part, store, buffers, semaphores):
        self.here, self.part, self.store = here, part, store
        self.point = Steps({k: call for k, call in enumerate(self.stages())}, SCATTER_STEPS)
        self.r0, self.rp, self.rd, self.rx, self.ry, self.r3 = buffers
        self.cs, self.cr, self.ps, self.pr, self.ds, self.dr = semaphores[:6]
        self.xs, self.xr, self.ys, self.yr, self.zs, self.zr = semaphores[6:]
        y, x, c, z = here
        self.sib = device_at(y, x, 1 - c, z)
        self.xn = device_at(y, 1 - x, c, z)
        self.yn = device_at(1 - y, x, c, z)
        self.partner = z + 1 - 2 * (z % 2)
        self.opposite = (z + 2) % 4
        self.zp = device_at(y, x, c, self.partner)
        self.copies = [[] for _ in part]

    def stages(self):
        return self.chip, self.pair, self.diagonal, self.sides, self.last

    def by_y(self, i):
        return ((0,), (2,)) if SUMMED_IN_PAIRS[i] else ((0, 2), (1, 3))

    def hop(self, i, kind, k):
        y, x, c, z = self.here
        part = self.part[i]
        if kind == "c":
            return part.at[:, :, 1 - c], self.r0[i], self.cs.at[i], self.cr.at[i], self.sib
        if kind == "p":
            block = (self.partner + 2 * k) % 4
            return part.at[1 - y, 1 - x, c, block], self.rp[i].at[k], self.ps.at[i, k], self.pr.at[i, k], self.zp
        if kind == "d":
            block = (z + k) % 4
            there = self.yn if k in self.by_y(i)[0] else self.xn
            return part.at[1 - y, 1 - x, c, block], self.rd[i].at[k], self.ds.at[i, k], self.dr.at[i, k], there
        if kind == "x":
            block = (z + k) % 4
            return part.at[y, 1 - x, c, block], self.rx[i].at[block], self.xs.at[i, k], self.xr.at[i, k], self.xn
        if kind == "y":
            block = (z + k) % 4
            return part.at[1 - y, x, c, block], self.ry[i].at[block], self.ys.at[i, k], self.yr.at[i, k], self.yn
        there = (z + k + 1) % 4
        return part.at[y, x, c, there], self.r3[i].at[k], self.zs.at[i, k], self.zr.at[i, k], device_at(y, x, c, there)

    def send(self, i, kind, *which):
        for k in which:
            remote(*self.hop(i, kind, k)).start()
            self.copies[i].append((kind, k))

    def wait(self, i, kind, *which):
        for k in which:
            remote(*self.hop(i, kind, k)).wait_recv()

    def drain(self, i):
        for kind, k in self.copies[i]:
            remote(*self.hop(i, kind, k)).wait_send()
        self.copies[i] = []

    def start(self, i):
        self.send(i, "c", 0)

    def chip(self, i):
        c = self.here[2]
        part, r0 = self.part[i], self.r0[i]
        self.wait(i, "c", 0)

        def add(k, _):
            a, b, q = k // 8, (k // 4) % 2, k % 4
            part[a, b, c, q] = part[a, b, c, q] + r0[a, b, q]
            return 0

        lax.fori_loop(0, 16, add, 0)
        first, second = self.by_y(i)
        if SUMMED_IN_PAIRS[i]:
            self.send(i, "p", 0, 1)
        else:
            self.send(i, "d", *first, *second)
        self.send(i, "x", *[k for k in (1, 3, 0, 2) if k not in first])
        self.send(i, "y", *[k for k in (0, 2, 1, 3) if k not in second])

    def pair(self, i):
        if not SUMMED_IN_PAIRS[i]:
            return
        y, x, c, z = self.here
        part = self.part[i]
        for k, block in enumerate((z, self.opposite)):
            self.wait(i, "p", k)
            part[1 - y, 1 - x, c, block] = part[1 - y, 1 - x, c, block] + self.rp[i][k]
            self.send(i, "d", 2 * k)

    def diagonal(self, i):
        y, x, c, z = self.here
        part = self.part[i]
        first, second = self.by_y(i)
        for k in first:
            self.wait(i, "d", k)
            block = (z + k) % 4
            part[y, 1 - x, c, block] = part[y, 1 - x, c, block] + self.rd[i][k]
            self.send(i, "x", k)
        for k in second:
            self.wait(i, "d", k)
            block = (z + k) % 4
            part[1 - y, x, c, block] = part[1 - y, x, c, block] + self.rd[i][k]
            self.send(i, "y", k)

    def sides(self, i):
        y, x, c, z = self.here
        part, rx, ry = self.part[i], self.rx[i], self.ry[i]
        self.wait(i, "x", 1, 2, 3, 0)
        self.wait(i, "y", 1, 3, 0, 2)

        def add(q, _):
            both = rx[q].astype(F32) + ry[q].astype(F32)
            part[y, x, c, q] = (part[y, x, c, q].astype(F32) + both).astype(BF16)
            return 0

        lax.fori_loop(0, 4, add, 0)
        self.send(i, "z", 1, 0, 2)

    def last(self, i):
        y, x, c, z = self.here
        self.wait(i, "z", 0, 1, 2)
        part, r3 = self.part[i], self.r3[i]
        total = (part[y, x, c, z].astype(F32) + r3[0].astype(F32)) + (r3[1].astype(F32) + r3[2].astype(F32))
        out, start, stride = self.store[i]
        flatten_into(out, total, start, stride)

    def rest(self):
        while self.point.table:
            self.point()


def flatten_into(out, value, start, stride):
    rows, size = value.shape
    for k in range(size // 128):
        out[pl.ds(start + k, rows, stride=stride), :] = value[:, k * 128 : (k + 1) * 128]


GRADS = ("down", "up", "pt", "qt", "ps", "qs")
WIDTHS = {"down": D, "up": FF, "pt": D, "qt": 3 * D, "ps": D, "qs": 3 * D}
ENTRIES = [("down", k * D // 2, D // 2) for k in range(2)] + [("up", k * FF // 2, FF // 2) for k in range(2)]
ENTRIES += [("pt", 0, D)] + [("qt", k * D, D) for k in range(3)] + [("ps", 0, D)] + [("qs", k * D, D) for k in range(3)]
DOWN, UP, PT, QT, PS, QS = 0, 2, 4, 5, 8, 9
SUMMED_IN_PAIRS = (True, True, True, True, False, False, True, True, True, False, True, False)
SCATTER_STEPS = (
    (), (), (), (), ((0, 0),), (), ((0, 1),), (), ((1, 0), (0, 2),), ((1, 1),), (), (), ((2, 0), (1, 2), (0, 3),),
    (), ((0, 4), (2, 1), (1, 4),), ((3, 0), (2, 2), (1, 3),), (), (), (), (), ((2, 4),), ((0, 5), (4, 0), (1, 5),),
    ((3, 1), (0, 6),), ((3, 2), (0, 7),), ((2, 3), (3, 4),), ((2, 5),), ((4, 1), (1, 6), (0, 8),), (),
    ((3, 3), (1, 7), (4, 2), (3, 5),), ((2, 6), (1, 8), (4, 4),), ((2, 7),), ((3, 6),),
    ((2, 8), (3, 7), (0, 9), (1, 9),), ((0, 10), (4, 3), (3, 8),), ((2, 9), (0, 11), (1, 11),), ((4, 5),), (), (),
    ((4, 6), (3, 9), (1, 10),), ((4, 7), (2, 11),), ((2, 10),), ((4, 8), (3, 11),), ((3, 10),), (), ((4, 9),), (),
    (), (), (), (), ((4, 11),), ((4, 10),),
)
BLOCKS = [("down", j) for j in range(4)] + [("up", j) for j in range(4)]
BLOCKS += [("pt", 0)] + [("qt", j) for j in range(3)] + [("ps", 0)] + [("qs", j) for j in range(3)]
SLOTS = 4


def attend_back(s, q, p, c_grad, first):
    def body(t, _):
        step = first + t
        item, pair = step // PAIRS, step % PAIRS
        rows = pl.ds(pl.multiple_of(item * TOKENS, TOKENS), TOKENS)
        at = [lane_cols(pair * 128 + j * D) for j in range(3)]
        soft = p[:, lane_cols(step * TOKENS, TOKENS)]
        dc = c_grad[rows, at[0]]
        queries, keys, values = (q[rows, where] for where in at)
        v_grad = pick_heads(t_dot(soft[:TOKENS], dc), t_dot(soft[TOKENS:], dc))
        soft_grad = dot_t(two_heads(dc, 1.0), values)
        wide = soft.astype(F32)
        product = soft_grad * wide
        score = (product - wide * jnp.sum(product, axis=-1, keepdims=True)).astype(BF16)
        q_both = dot(score, keys)
        q_grad = pick_heads(q_both[:TOKENS], q_both[TOKENS:]) * HD ** (-0.5)
        k_grad = pick_heads(t_dot(score[:TOKENS], queries), t_dot(score[TOKENS:], queries)) * HD ** (-0.5)
        q[rows, at[0]] = q_grad.astype(BF16)
        q[rows, at[1]] = k_grad.astype(BF16)
        q[rows, at[2]] = v_grad.astype(BF16)
        return 0

    lax.fori_loop(0, PAIRS // 2, body, 0)


def backward_kernel(names, *refs):
    s = Names(names, refs)
    here = place()
    y, x, c, z = here
    me = ((y * 2 + x) * 2 + c) * 4 + z
    loads = {}

    def fetch(name, src, dst, k):
        loads[name] = pltpu.make_async_copy(src, dst, s.load_sem.at[k])
        loads[name].start()

    def have(*wanted):
        for name in wanted:
            loads.pop(name).wait()

    def fetch_block(k):
        tensor, j = BLOCKS[k]
        src = getattr(s, "w_" + tensor)
        src = src.at[j] if tensor == "down" else src.at[:, :, pl.ds(j * D, D)]
        pltpu.make_async_copy(src, s.blocks.at[k % SLOTS], s.load_sem.at[16 + k % SLOTS]).start()

    def block(k):
        slot = k % SLOTS
        pltpu.make_async_copy(s.w_ps, s.blocks.at[slot], s.load_sem.at[16 + slot]).wait()
        return s.blocks[slot].reshape(D, D)

    def used(k):
        if k + SLOTS < len(BLOCKS):
            fetch_block(k + SLOTS)

    def used_at(first, j, count):
        for k in range(count):
            if first + k + SLOTS < len(BLOCKS):
                @pl.when(j == k)
                def _(k=k):
                    fetch_block(first + k + SLOTS)

    fetch("g", s.in_g, s.g, 0)
    fetch("mods", s.in_mods, s.mods, 1)
    fetch_block(0)
    fetch_block(1)
    fetch("gp", s.in_gp, s.gp, 2)
    fetch("h3", s.in_h3, s.h3, 3)
    fetch_block(2)
    fetch_block(3)
    fetch("n3", s.in_n3, s.n3, 4)
    fetch("r3", s.in_r3, s.r3, 5)

    def fetch_rest(k):
        for i, (name, dst) in enumerate((("a", s.a), ("c", s.c), ("h", s.h), ("n", s.n), ("r", s.r))):
            fetch(name, getattr(s, f"in_{name}{k}"), dst, 6 + i)

    fetch_rest(2)

    homes = {"down": (s.b0, 0), "up": (s.b1, 0), "pt": (s.b2, 0), "qt": (s.b2, D), "ps": (s.b3, 0), "qs": (s.b3, D)}
    parts, store = [], []
    for t, start, width in ENTRIES:
        ref, base = homes[t]
        parts.append(ref.at[:, :, :, :, :, pl.ds(base + start, width)])
        store.append((getattr(s, "grad_" + t), start // 128, WIDTHS[t] // 128))
    buffers = [[getattr(s, f"r{k}_{i}") for i in range(len(ENTRIES))] for k in range(6)]
    scatter = Scatter(here, parts, store, buffers, [getattr(s, f"ss{k}") for k in range(12)])
    sender = Sender()
    little = Gather(here, sender, [s.small], [s.small_all], [getattr(s, f"ls{i}") for i in range(8)], s.ls8)

    barrier = pltpu.get_barrier_semaphore()
    partners = [device_at(y, x, 1 - c, z), device_at(y, 1 - x, c, z), device_at(1 - y, x, c, z)]
    partners += [device_at(y, x, c, (z + step) % 4) for step in (1, 2, 3)]
    for partner in partners:
        pl.semaphore_signal(barrier, inc=1, device_id=partner, device_id_type=MESH)
    pl.semaphore_wait(barrier, 6)

    s.rows[...] = jnp.zeros_like(s.rows)
    valid_rows(s)
    ones = jnp.ones((8, 2 * TOKENS), BF16)
    have("mods")
    for item in range(2):
        gate = s.mods[8, item : item + 1, :]

        def first(t, _):
            rows = rows_of(item, t, CHUNK)
            d3 = s.cotangent[rows, :].astype(F32) * s.valid[rows, :]
            s.d[rows, :] = d3
            s.dm[rows, :] = (gate * d3).astype(BF16)
            return 0

        lax.fori_loop(0, TOKENS // CHUNK, first, 0)
        s.rows[9 * item + 8 : 9 * item + 9, :] = s.dga3[item : item + 1, :]
    s.rows[22:23, :] = dot(ones, s.dm[...])[:1]

    have("g")

    def starts(first, indices):
        return {at: lambda i=first + n: scatter.start(i) for n, at in enumerate(indices)}

    def down(t):
        k, j = t // 2, t % 2
        cols = lane_cols(k * (D // 2), D // 2)
        grad = t_dot(s.g[:, lane_cols(2 * j * D, 2 * D)], s.dm[:, cols]).astype(BF16)
        s.b0[j, :, :, :, :, cols] = grad.reshape(2, 2, 4, 4 * D // DEVICES, D // 2)

    scatter.point.rolled(4, (down, starts(DOWN, (1, 3)), 2))
    fetch("p", s.in_p2, s.g, 0)

    have("gp", "h3")

    def up_back(j):
        cols = lane_cols(j * D, D)
        s.acc[...] = dot_t(s.dm[...], block(j))
        used_at(0, j, 4)

        def slope(t, _):
            rows = rows_of(0, t, CHUNK)
            s.gp[rows, cols] = (s.acc[rows, :] * s.gp[rows, cols].astype(F32)).astype(BF16)
            return 0

        lax.fori_loop(0, 2 * TOKENS // CHUNK, slope, 0)
        s.rows[pl.ds(18 + j, 1), :] = dot(ones, s.gp[:, cols])[:1]

    def up_grad(j):
        cols = lane_cols(j * D, D)
        grad = t_dot(s.h3[...], s.gp[:, cols]).astype(BF16)
        s.b1[:, :, :, :, :, cols] = grad.reshape(2, 2, 2, 4, D // DEVICES, D)

    scatter.point.rolled(4, (up_back, {}, 1), (up_grad, starts(UP, (1, 3)), 1))

    def back_through(first_block, source, count, every):
        s.acc[...] = jnp.zeros_like(s.acc)

        def body(j):
            s.acc[...] = s.acc[...] + dot_t(source[:, lane_cols(j * D, D)], block(first_block + j))
            used_at(first_block, j, count)

        scatter.point.rolled(count, (body, {}, every))

    def qkv_grad(out, j):
        grad = t_dot(s.h[...], s.gp[:, lane_cols(j * D, D)]).astype(BF16)
        out[:, :, :, :, :, lane_cols(D + j * D, D)] = grad.reshape(2, 2, 2, 4, D // DEVICES, D)

    back_through(4, s.gp, 4, 2)
    fetch("q", s.in_q2, s.gp.at[:, pl.ds(0, 3 * D)], 2)

    def norm_back(n_ref, r_ref, base, a_ref, gate_row, between=False):
        for item in range(2):
            scale = 1.0 + s.mods[base + 1, item : item + 1, :]
            gate = None if gate_row is None else s.mods[gate_row, item : item + 1, :]

            def body(t, totals):
                rows = rows_of(item, t, CHUNK)
                dh, n = s.acc[rows, :], n_ref[rows, :].astype(F32)
                g = dh * scale
                dhn = dh * n
                mean_g = jnp.mean(g, axis=-1, keepdims=True)
                mean_gn = jnp.mean(g * n, axis=-1, keepdims=True)
                d = s.d[rows, :] + r_ref[rows, :] * (g - mean_g - n * mean_gn)
                s.d[rows, :] = d
                fold = lambda v: jnp.sum(v.reshape(CHUNK // 8, 8, D), axis=0)
                new = [totals[0] + fold(dh), totals[1] + fold(dhn)]
                if gate is not None:
                    s.dm[rows, :] = (gate * d).astype(BF16)
                    new.append(totals[2] + fold(d * a_ref[rows, :].astype(F32)))
                return tuple(new)

            count = 2 if gate is None else 3
            totals = lax.fori_loop(0, TOKENS // CHUNK, body, (jnp.zeros((8, D), F32),) * count)
            for where, total in zip((base, base + 1, base - 1), totals):
                row = 9 * item + where
                s.rows[row : row + 1, :] = jnp.sum(total, axis=0, keepdims=True)
            if between or item:
                scatter.point()

    have("n3", "r3", "a")
    norm_back(s.n3, s.r3, 6, s.a, 5)
    have("c")
    s.b2[:, :, :, :, :, :D] = t_dot(s.c[...], s.dm[...]).astype(BF16).reshape(2, 2, 2, 4, D // DEVICES, D)
    scatter.start(PT)
    s.dc[...] = dot_t(s.dm[...], block(8)).astype(BF16)
    used(8)
    scatter.point()
    have("q", "p")
    scatter.point.rolled(4, (lambda k: attend_back(s, s.gp, s.g, s.dc, 3 * k), {}, 1))
    fetch("p", s.in_p1, s.g, 0)
    have("h")
    scatter.point.rolled(3, (lambda j: qkv_grad(s.b2, j), starts(QT, (0, 1, 2)), 1))
    back_through(9, s.gp, 3, 1)
    fetch("q", s.in_q1, s.gp.at[:, pl.ds(0, 3 * D)], 2)
    have("n", "r")
    fetch("c", s.in_c1, s.c, 7)
    fetch("h", s.in_h1, s.h, 8)
    fetch("a", s.in_a1, s.a, 6)
    have("a")
    norm_back(s.n, s.r, 3, s.a, 2)
    fetch("n", s.in_n1, s.n, 9)
    fetch("r", s.in_r1, s.r, 10)
    have("c")
    s.b3[:, :, :, :, :, :D] = t_dot(s.c[...], s.dm[...]).astype(BF16).reshape(2, 2, 2, 4, D // DEVICES, D)
    scatter.start(PS)
    s.dc[...] = dot_t(s.dm[...], block(12)).astype(BF16)
    used(12)
    scatter.point()
    have("q", "p")
    scatter.point.rolled(4, (lambda k: attend_back(s, s.gp, s.g, s.dc, 3 * k), {}, 1))
    have("h")
    scatter.point.rolled(3, (lambda j: qkv_grad(s.b3, j), starts(QS, (0, 1, 2)), 1))
    back_through(13, s.gp, 3, 1)
    have("n", "r")
    norm_back(s.n, s.r, 0, None, None, True)
    s.small[...] = s.rows[...].astype(BF16)
    little.start(0)
    scatter.point()
    little.stage1(0)
    scatter.point()
    little.stage2(0)
    scatter.point()
    little.stage3(0)
    scatter.point()
    little.finish(0)

    spot = lax.broadcasted_iota(jnp.int32, (D, 128), 0) % (D // DEVICES)

    def ada_grad(j):
        chosen = jnp.where((spot == j) | (spot == j + 9), s.chosen[...], jnp.zeros((D, 128), BF16))
        grad = t_dot(chosen, s.small_all[...].reshape(D, D))[: D // DEVICES]
        flatten_into(s.grad_ada, grad, j * (D // 128), 9 * D // 128)

    scatter.point.rolled(9, (ada_grad, {}, 1))
    gathered = s.small_all[...].reshape(D, D)
    row = lax.broadcasted_iota(jnp.int32, (16, D), 0)
    slot = lax.broadcasted_iota(jnp.int32, (16, D), 1) % (D // DEVICES)
    take = ((row < 9) & ((slot == row) | (slot == row + 9))) | ((row >= 9) & (slot == row + 9))
    s.grad_bias[...] = dot(take.astype(F32).astype(BF16), gathered)
    scatter.rest()
    for i in range(len(ENTRIES)):
        scatter.drain(i)
    sender.drain()


def run_backward(cotangent, buckets, dga3, chosen, kept):
    vmem, any_space = pl.BlockSpec(memory_space=pltpu.VMEM), pl.BlockSpec(memory_space=pl.ANY)
    rows, part = 2 * TOKENS, D // DEVICES
    ins = {"cotangent": cotangent, "buckets": buckets, "dga3": dga3, "chosen": chosen}
    fetched = {"in_" + name: kept[name] for name in save_shapes(TOKENS)}
    for t in GRADS:
        shape = (4, DEVICES, part, D) if t == "down" else (DEVICES, part, WIDTHS[t])
        fetched["w_" + t] = kept["w_" + t].reshape(shape)
    ins |= fetched
    block_of = [(4 * part if t == "down" else part, width) for t, _, width in ENTRIES]
    outs = {"grad_" + t: (DEVICES * part * WIDTHS[t] * (4 if t == "down" else 1) // DEVICES // 128, 128) for t in GRADS}
    outs |= {"grad_ada": (part * 9 * D // 128, 128), "grad_bias": (16, D), "d": (rows, D)}
    dma = pltpu.SemaphoreType.DMA
    big = lambda *block: pltpu.VMEM((2, 2, 2, 4) + block, BF16)
    scratch = {
        "b0": big(4 * part, D), "b1": big(part, FF), "b2": big(part, FF), "b3": big(part, FF),
        "blocks": pltpu.VMEM((SLOTS, DEVICES, part, D), BF16),
        "g": pltpu.VMEM((rows, FF), BF16), "gp": pltpu.VMEM((rows, FF), BF16),
        "acc": pltpu.VMEM((rows, D), F32),
        "mods": pltpu.VMEM((9, 8, D), F32), "rows": pltpu.VMEM((24, D), F32),
        "small": pltpu.VMEM((24, D), BF16), "small_all": big(24, D),
        "r3": pltpu.VMEM((rows, 1), F32), "r": pltpu.VMEM((rows, 1), F32), "valid": pltpu.VMEM((rows, 1), F32),
        "load_sem": dma((16 + SLOTS,)),
    }
    scratch |= {name: pltpu.VMEM((rows, D), BF16) for name in ("dm", "dc", "h3", "n3", "a", "c", "h", "n")}
    for k, lead in enumerate(Scatter.LEADING):
        scratch |= {f"r{k}_{i}": pltpu.VMEM(lead + block, BF16) for i, block in enumerate(block_of)}
    scratch |= {f"ss{k}": dma((len(ENTRIES),) + extra) for k, extra in enumerate(Scatter.SEMAPHORES)}
    scratch |= {f"ls{i}": kind for i, kind in enumerate(Gather.scratch(1))}
    names = list(ins) + list(outs) + list(scratch)
    results = pl.pallas_call(
        lambda *refs: backward_kernel(names, *refs),
        out_shape=tuple(jax.ShapeDtypeStruct(shape, F32) for shape in outs.values()),
        in_specs=[vmem] * 4 + [any_space] * len(fetched),
        out_specs=(vmem,) * len(outs),
        scratch_shapes=list(scratch.values()),
        compiler_params=pltpu.CompilerParams(
            collective_id=2, has_side_effects=True, vmem_limit_bytes=VMEM_LIMIT
        ),
        name="backward",
    )(*ins.values())
    return dict(zip(outs, results))


def deliver_kernel(count, *refs):
    src, out, buf = refs[:count], refs[count : 2 * count], refs[2 * count : 3 * count]
    coming, going = refs[3 * count :]
    copies = []
    for i in sorted(range(count), key=lambda i: -math.prod(src[i].shape)):
        rows = src[i].shape[0]
        step = rows // 2 if rows >= 512 else rows
        for start in range(0, rows, step):
            at = pl.ds(start, min(step, rows - start))
            k = len(copies)
            copies.append((
                pltpu.make_async_copy(src[i].at[at], buf[i].at[at], coming.at[k]),
                pltpu.make_async_copy(buf[i].at[at], out[i].at[at], going.at[k]),
            ))
    for first, _ in copies:
        first.start()
    for first, second in copies:
        first.wait()
        second.start()
    for _, second in copies:
        second.wait()


def deliver(results):
    count = len(results)
    any_space = pl.BlockSpec(memory_space=pl.ANY)
    dma = pltpu.SemaphoreType.DMA((2 * count + 2,))
    return pl.pallas_call(
        lambda *refs: deliver_kernel(count, *refs),
        out_shape=tuple(jax.ShapeDtypeStruct(r.shape, r.dtype) for r in results),
        in_specs=[any_space] * count,
        out_specs=(any_space,) * count,
        scratch_shapes=[pltpu.VMEM(r.shape, r.dtype) for r in results] + [dma, dma],
        compiler_params=pltpu.CompilerParams(vmem_limit_bytes=VMEM_LIMIT),
        name="deliver",
    )(*results)


def norm_parts(rows):
    centre = rows - jnp.mean(rows, axis=-1, keepdims=True)
    inverse = lax.rsqrt(jnp.mean(centre * centre, axis=-1, keepdims=True) + EPS)
    return centre * inverse, inverse


def norm_back(grad, normed, inverse, scale):
    shift_grad = jnp.sum(grad, axis=1)
    scale_grad = jnp.sum(grad * normed, axis=1)
    pulled = grad * (1.0 + scale)
    back = inverse * (
        pulled
        - jnp.mean(pulled, axis=-1, keepdims=True)
        - normed * jnp.mean(pulled * normed, axis=-1, keepdims=True)
    )
    return back, shift_grad, scale_grad


def heads(x):
    return x.reshape(x.shape[0], x.shape[1], HEADS, HD)


def attention(low, qkv_w, proj_w, mask):
    packed = dot(low, qkv_w).astype(BF16)
    q, k, v = (heads(part) for part in jnp.split(packed, 3, axis=-1))
    scores = jnp.einsum("bqhd,bkhd->bhqk", q, k, preferred_element_type=F32) * HD ** (-0.5)
    scores = jnp.where(mask, scores, MASKED)
    soft = jax.nn.softmax(scores, axis=-1)
    context = jnp.einsum("bhqk,bkhd->bqhd", soft.astype(BF16), v, preferred_element_type=F32)
    context = context.astype(BF16).reshape(low.shape)
    return dot(context, proj_w), (q, k, v, soft, context)


def attention_back(grad_low, low, qkv_w, proj_w, kept):
    q, k, v, soft, context = kept
    proj_grad = jnp.einsum("bld,ble->de", context, grad_low, preferred_element_type=F32)
    ctx = heads(jnp.einsum("ble,de->bld", grad_low, proj_w, preferred_element_type=F32).astype(BF16))
    v_grad = jnp.einsum("bhqk,bqhd->bkhd", soft.astype(BF16), ctx, preferred_element_type=F32)
    soft_grad = jnp.einsum("bqhd,bkhd->bhqk", ctx, v, preferred_element_type=F32)
    row_dot = jnp.sum(soft_grad * soft, axis=-1, keepdims=True)
    score_grad = (soft * (soft_grad - row_dot)).astype(BF16)
    q_grad = jnp.einsum("bhqk,bkhd->bqhd", score_grad, k, preferred_element_type=F32) * HD ** (-0.5)
    k_grad = jnp.einsum("bhqk,bqhd->bkhd", score_grad, q, preferred_element_type=F32) * HD ** (-0.5)
    packed = jnp.concatenate(
        [part.astype(BF16).reshape(low.shape) for part in (q_grad, k_grad, v_grad)], axis=-1
    )
    qkv_grad = jnp.einsum("bld,ble->de", low, packed, preferred_element_type=F32)
    low_grad = jnp.einsum("ble,de->bld", packed, qkv_w, preferred_element_type=F32)
    return low_grad, qkv_grad, proj_grad


def gather_plain(shards):
    return tuple(lax.all_gather(s, AXES, axis=0) for s in shards)


def scatter_plain(parts, small):
    devices = lax.axis_size(AXES)
    sums = tuple(
        lax.psum_scatter(p.reshape((devices,) + p.shape[-2:]), AXES, scatter_dimension=0, tiled=True)[
            0
        ].astype(F32)
        for p in parts
    )
    return sums + (lax.all_gather(small, AXES, axis=0),)


def per_device_plain(latents, buckets, step_ids, qs, ps, qt, pt, up, down, ada, biases, cotangent):
    devices = lax.axis_size(AXES)
    micro = latents.shape[0]
    frames, spatial = latents.shape[2], latents.shape[3]
    tokens = frames * spatial
    rows = D // devices

    gather, scatter = gather_plain, scatter_plain

    ada_columns = lax.all_to_all(
        ada.reshape(rows, 9 * D), AXES, split_axis=1, concat_axis=0, tiled=True
    )
    own_bias = jnp.pad(biases, (0, D - biases.shape[0]))[None]
    small = jnp.concatenate([timestep_condition(step_ids[:, 0]), own_bias], axis=0)
    shards = [small] + [w.reshape(rows, -1) for w in (qs, ps, qt, pt, up)] + [down.reshape(-1, D)]
    small, *gathered = gather(shards)
    w_qs, w_ps, w_qt, w_pt, w_up = (w.reshape(D, -1) for w in gathered[:5])
    w_down = gathered[5].reshape(-1, D)
    small = small.reshape(devices, micro + 1, D)
    condition = small[:, :micro].reshape(devices * micro, D)
    bias = small[:, micro, : biases.shape[0]].reshape(-1).astype(F32)
    modulation = lax.all_to_all(
        dot(condition, ada_columns), AXES, split_axis=0, concat_axis=1, tiled=True
    )
    modulation = (modulation + bias[: 9 * D]).reshape(micro, 9, 1, D)
    b_up, b_down = bias[9 * D : 9 * D + FF], bias[9 * D + FF :]

    positions = jnp.arange(tokens)
    frame, place = positions // spatial, positions % spatial
    bucket = buckets[:, 0]
    length = jnp.where(bucket == 0, spatial, jnp.where(bucket == 1, spatial // 2, spatial // 8))
    valid = place[None, :] < length[:, None]
    space_mask = (frame[:, None] == frame[None, :])[None, None] & valid[:, None, None, :]
    time_mask = (place[:, None] == place[None, :])[None, None]
    valid_rows = valid.astype(F32)[:, :, None]

    sh1, sc1, ga1, sh2, sc2, ga2, sh3, sc3, ga3 = (modulation[:, i] for i in range(9))
    x = latents.reshape(micro, tokens, D).astype(F32)
    n1, r1 = norm_parts(x)
    h1 = (n1 * (1.0 + sc1) + sh1).astype(BF16)
    a1, kept1 = attention(h1, w_qs, w_ps, space_mask)
    x1 = x + ga1 * a1
    n2, r2 = norm_parts(x1)
    h2 = (n2 * (1.0 + sc2) + sh2).astype(BF16)
    a2, kept2 = attention(h2, w_qt, w_pt, time_mask)
    x2 = x1 + ga2 * a2
    n3, r3 = norm_parts(x2)
    h3 = (n3 * (1.0 + sc3) + sh3).astype(BF16)
    hidden = dot(h3, w_up) + b_up
    gelu, pull = jax.vjp(lambda u: jax.nn.gelu(u, approximate=True), hidden)
    g = gelu.astype(BF16)
    m = dot(g, w_down) + b_down
    x3 = x2 + ga3 * m
    output = (x3 * valid_rows).astype(BF16)

    d3 = cotangent.reshape(micro, tokens, D).astype(F32) * valid_rows
    dm = (ga3 * d3).astype(BF16)
    dga3 = jnp.sum(d3 * m, axis=1)
    db_down = jnp.sum(dm.astype(F32), axis=(0, 1))
    dw_down = jnp.einsum("bsk,bsd->kd", g, dm, preferred_element_type=F32)
    dg = jnp.einsum("bsd,kd->bsk", dm, w_down, preferred_element_type=F32)
    du = pull(dg)[0].astype(BF16)
    db_up = jnp.sum(du.astype(F32), axis=(0, 1))
    dw_up = jnp.einsum("bsd,bsk->dk", h3, du, preferred_element_type=F32)
    dh3 = jnp.einsum("bsk,dk->bsd", du, w_up, preferred_element_type=F32)
    dv, dsh3, dsc3 = norm_back(dh3, n3, r3, sc3)
    d2 = d3 + dv
    da2 = (ga2 * d2).astype(BF16)
    dga2 = jnp.sum(d2 * a2, axis=1)
    dh2, dw_qt, dw_pt = attention_back(da2, h2, w_qt, w_pt, kept2)
    dv, dsh2, dsc2 = norm_back(dh2, n2, r2, sc2)
    d1 = d2 + dv
    da1 = (ga1 * d1).astype(BF16)
    dga1 = jnp.sum(d1 * a1, axis=1)
    dh1, dw_qs, dw_ps = attention_back(da1, h1, w_qs, w_ps, kept1)
    dv, dsh1, dsc1 = norm_back(dh1, n1, r1, sc1)
    latents_grad = d1 + dv

    dmod = jnp.stack([dsh1, dsc1, dga1, dsh2, dsc2, dga2, dsh3, dsc3, dga3], axis=1)
    small = jnp.concatenate(
        [dmod.reshape(micro * 9, D), db_up.reshape(-1, D), db_down.reshape(-1, D)], axis=0
    ).astype(BF16)
    parts = [
        part.astype(BF16).reshape(tuple(gathered[i].shape))
        for i, part in ((5, dw_down), (4, dw_up), (3, dw_pt), (2, dw_qt), (1, dw_ps), (0, dw_qs))
    ]
    ddown, dup, dpt, dqt, dps, dqs, small = scatter(parts, small)
    flat = tuple(part.reshape(-1) for part in (dqs, dps, dqt, dpt, dup))
    small = small.reshape(devices, -1, D)
    dmod_all = small[:, : micro * 9].reshape(devices * micro, 9 * D)
    me = lax.axis_index(AXES)
    my_condition = lax.dynamic_slice_in_dim(condition, me * rows, rows, axis=1)
    dw_ada = lax.dot_general(
        my_condition, dmod_all, (((0,), (0,)), ((), ())), preferred_element_type=F32
    )
    db = jnp.concatenate(
        [
            jnp.sum(dmod_all.astype(F32), axis=0),
            jnp.sum(small[:, micro * 9 :].astype(F32), axis=0).reshape(-1),
        ]
    )
    db = lax.dynamic_slice_in_dim(db, me * biases.shape[0], biases.shape[0])

    shape = latents.shape
    return (
        output.reshape(shape),
        latents_grad.reshape(shape),
        *flat,
        ddown.reshape(-1),
        dw_ada.reshape(-1),
        db,
    )


def per_device(latents, buckets, step_ids, qs, ps, qt, pt, up, down, ada, biases, cotangent):
    rows = 2 * TOKENS
    conditions = timestep_condition(step_ids[:, 0])
    shards = [w.reshape(-1, 128) for w in (qs, ps, qt, pt, up, down)]
    tokens = latents.reshape(rows, D)
    grads_in = cotangent.reshape(rows, D)
    output, dga3, chosen, kept = run_forward(
        conditions, biases.reshape(1, -1), buckets, ada.reshape(-1, 128), shards, tokens, grads_in
    )
    grads = run_backward(grads_in, buckets, dga3, chosen, kept)
    me = lax.axis_index(AXES)
    bias_grad = grads["grad_bias"][:14].reshape(-1)
    names = ["d"] + ["grad_" + t for t in ("qs", "ps", "qt", "pt", "up", "down", "ada")]
    output, latents_grad, *flat = deliver([output] + [grads[name] for name in names])
    return (
        output.reshape(latents.shape),
        latents_grad.reshape(latents.shape),
        *(g.reshape(-1) for g in flat),
        lax.dynamic_slice_in_dim(bias_grad, me * SHARE, SHARE),
    )


def solution(mesh):
    items = P(None, AXES, None, None, None)
    flat = P(AXES)
    known = mesh.shape["wide"] == 8 and mesh.shape["narrow"] == 4
    return jax.shard_map(
        per_device if known else per_device_plain,
        mesh=mesh,
        in_specs=(items, P(None, AXES), P(None, AXES)) + (flat,) * 8 + (items,),
        out_specs=(items, items) + (flat,) * 8,
        check_vma=False,
    )
```

profile of v0, /device:TPU:0, one launch (start us, length us, event | category | flops | bytes accessed | tf_op | source)
XLA Modules:
  0.0 236.4 jit_solution(10262151296610024740)
XLA Ops:
  0.7 0.7 convert_bitcast_fusion
  1.3 0.1 multiply_cosine_fusion
  1.4 0.6 fusion.refs_0_
  2.0 1.2 reshape.103.refs_1_
  3.3 1.3 copy.22.refs_2_.refs_1_
  4.6 115.9 %forward.1 = (bf16[512,768]{1,0:T(8,128)(2,1)}, f32[2,768]{1,0:T(2,128)}, bf16[768,128]{1,0:T(8,128)(2,1)}, bf16[512,768]{1,0:T(8,128)(2,1)}, f32[512,1]{1,0:T(8...) custom-call(bf16[2,768]{1,0:T(2,128)(2,1)} %fusion.refs_0_, ...), custom_call_target="tpu_custom_call" | custom-call | tf_op jit(solution)/shard_map/forward/pallas_call | solution.py:766
  120.5 110.7 %backward.1 = (f32[576,128]{1,0:T(8,128)}, f32[576,128]{1,0:T(8,128)}, f32[144,128]{1,0:T(8,128)}, f32[432,128]{1,0:T(8,128)}, f32[144,128]{1,0:T(8,128)}, /*ind...) custom-call(bf16[512,768]{1,0:T(8,128)(2,1)} %bitcast.36, ...), custom_call_target="tpu_custom_call" | custom-call | tf_op jit(solution)/shard_map/backward/pallas_call | solution.py:1233
  231.2 3.8 %deliver.1 = (bf16[512,768]{1,0:T(8,128)(2,1)}, f32[512,768]{1,0:T(8,128)}, f32[432,128]{1,0:T(8,128)}, f32[144,128]{1,0:T(8,128)}, f32[432,128]{1,0:T(8,128)}, ...) custom-call(bf16[512,768]{1,0:T(8,128)(2,1)} %get-tuple-element.57.refs_0_, ...), custom_call_target="tpu_custom_call" | custom-call | tf_op jit(solution)/shard_map/deliver/pallas_call | solution.py:1274
  235.0 0.8 reshape.128
  235.8 0.7 dynamic_slice.3
  (1 shorter events, 0.0 us)
where the time goes:
time: 237 us; the launch traced here: 236 us
  Pallas kernels  230 us (97%)
  local copies, waits for them, and re-layouts  3.99 us (2%)
    pallas_call x1, Pallas kernels, run_forward(): pl.pallas_call(lambda *refs: forward_kernel(names, *refs), out_shape=(jax...  116 us
    pallas_call x1, Pallas kernels, run_backward(): pl.pallas_call(lambda *refs: backward_kernel(names, *refs), out_shape=tup...  111 us

commit v1 on v0

--- a/solution.py
+++ b/solution.py
@@ -284,13 +284,13 @@
 
 PAIRED = (True, True, False, True, True, True, False, False)
 SPREAD_STEPS = (
-    (("A", 0), ("B", 0), ("A", 6),), (), (), (), (("A", 2),), (), (("A", 4), ("A", 7),), (), (),
-    (("A", 1), ("B", 1), ("A", 3),), (), (("C", 0),), (("B", 2),), (), (("B", 4),), (("B", 3), ("C", 1),), (), (),
+    (("A", 0), ("B", 0),), (), (), (("A", 1), ("A", 2), ("A", 3),), (("A", 6),), (("A", 4),), (), (("A", 5),), (),
+    (("B", 1),), (("B", 2),), (("C", 0),), (), (("B", 4),), (("B", 3),), (("C", 1),), (), (),
     (("X", 0), ("X", 1), ("C", 2), ("D", 0), ("D", 1), ("C", 4), ("P", 0),),
-    (("B", 5), ("B", 6), ("P", 1), ("X", 2), ("C", 3),), (), (), (("B", 7), ("X", 4),), (),
-    (("D", 2), ("A", 5), ("C", 5),), (("X", 3),), (), (("D", 4),), (), (("C", 6),), (), (),
-    (("X", 5), ("P", 4), ("D", 3),), (("C", 7),), (("P", 3),), (("D", 5), ("X", 6),), (), (), (),
-    (("P", 5), ("X", 7),), (), (), (("D", 6),), (("D", 7),), (), (),
+    (("B", 5), ("P", 1), ("X", 2), ("C", 3),), (), (), (("B", 6), ("X", 4),), (), (), (("D", 2), ("C", 5),), (),
+    (("B", 7), ("X", 3), ("D", 4),), (), (), (("C", 6),), (), (("D", 3), ("X", 5),), (),
+    (("A", 7), ("C", 7), ("P", 4), ("X", 6),), (("P", 3), ("D", 5),), (), (), (), (("P", 5), ("X", 7),), (), (),
+    (("D", 6),), (("D", 7),), (), (),
 )
 
 
@@ -745,7 +745,7 @@
     scratch |= {"own_" + t: pltpu.VMEM(shape, BF16) for t, shape in own.items()}
     scratch |= {
         "small": pltpu.VMEM((8, D), BF16), "little": pltpu.VMEM((8, D), F32),
-        "stage": pltpu.VMEM(ada.shape, F32), "ada": pltpu.VMEM((part, 9 * D), BF16),
+        "stage": pltpu.VMEM((ada.shape[0] + 64, 128), F32), "ada": pltpu.VMEM((part, 9 * D), BF16),
         "valid": pltpu.VMEM((rows, 1), F32),
         "small_all": pltpu.VMEM((2, 2, 2, 4, 8, D), BF16),
         "ada_cols": pltpu.VMEM((DEVICES, part, 256), BF16),
@@ -923,15 +923,15 @@
 ENTRIES = [("down", k * D // 2, D // 2) for k in range(2)] + [("up", k * FF // 2, FF // 2) for k in range(2)]
 ENTRIES += [("pt", 0, D)] + [("qt", k * D, D) for k in range(3)] + [("ps", 0, D)] + [("qs", k * D, D) for k in range(3)]
 DOWN, UP, PT, QT, PS, QS = 0, 2, 4, 5, 8, 9
-SUMMED_IN_PAIRS = (True, True, True, True, False, False, True, True, True, False, True, False)
+SUMMED_IN_PAIRS = (False, False, False, True, True, True, True, False, False, False, False, False)
 SCATTER_STEPS = (
-    (), (), (), (), ((0, 0),), (), ((0, 1),), (), ((1, 0), (0, 2),), ((1, 1),), (), (), ((2, 0), (1, 2), (0, 3),),
-    (), ((0, 4), (2, 1), (1, 4),), ((3, 0), (2, 2), (1, 3),), (), (), (), (), ((2, 4),), ((0, 5), (4, 0), (1, 5),),
-    ((3, 1), (0, 6),), ((3, 2), (0, 7),), ((2, 3), (3, 4),), ((2, 5),), ((4, 1), (1, 6), (0, 8),), (),
-    ((3, 3), (1, 7), (4, 2), (3, 5),), ((2, 6), (1, 8), (4, 4),), ((2, 7),), ((3, 6),),
-    ((2, 8), (3, 7), (0, 9), (1, 9),), ((0, 10), (4, 3), (3, 8),), ((2, 9), (0, 11), (1, 11),), ((4, 5),), (), (),
-    ((4, 6), (3, 9), (1, 10),), ((4, 7), (2, 11),), ((2, 10),), ((4, 8), (3, 11),), ((3, 10),), (), ((4, 9),), (),
-    (), (), (), (), ((4, 11),), ((4, 10),),
+    (), (), (), ((0, 0), (1, 0),), (), ((0, 1), (1, 1),), ((2, 0),), (), ((0, 2), (1, 2),), (), ((2, 1),), (),
+    ((0, 3), (3, 0),), (), ((0, 4), (1, 3), (2, 2),), (), ((3, 1), (4, 0),), ((1, 4),), (), (), (), ((0, 5),), (),
+    ((0, 6), (2, 3), (4, 1), (0, 7), (1, 5), (1, 7),), ((1, 6), (2, 4), (3, 2),), (), ((0, 8), (3, 3), (1, 8),),
+    ((2, 7),), ((2, 6), (2, 5), (3, 4), (4, 2),), ((2, 8),), (), ((3, 7), (3, 6), (4, 3), (3, 5), (0, 9), (1, 9),),
+    ((3, 8), (4, 4), (0, 10), (1, 10),), ((2, 9),), ((0, 11), (4, 7), (1, 11),), (), ((2, 10), (4, 6),), (),
+    ((3, 9), (4, 5), (2, 11),), (), ((3, 10), (4, 8),), ((3, 11), (4, 9),), (), (), (), (), ((4, 10),), (), (), (),
+    (), ((4, 11),),
 )
 BLOCKS = [("down", j) for j in range(4)] + [("up", j) for j in range(4)]
 BLOCKS += [("pt", 0)] + [("qt", j) for j in range(3)] + [("ps", 0)] + [("qs", j) for j in range(3)]

time: 237 us -> 234 us (0.987)
  no operation moved by 1% of the time
where the time goes in v1:
time: 234 us
  Pallas kernels  228 us (97%)
  local copies, waits for them, and re-layouts  3.99 us (2%)
    pallas_call x1, Pallas kernels, run_forward(): pl.pallas_call(lambda *refs: forward_kernel(names, *refs), out_shape=(jax...  115 us
    pallas_call x1, Pallas kernels, run_backward(): pl.pallas_call(lambda *refs: backward_kernel(names, *refs), out_shape=tup...  109 us

profile of v1, /device:TPU:0, one launch (start us, length us, event | category | flops | bytes accessed | tf_op | source)
XLA Modules:
  0.0 233.7 jit_solution(9520737664446390283)
XLA Ops:
  0.7 0.7 convert_bitcast_fusion
  1.3 0.1 multiply_cosine_fusion
  1.4 0.6 fusion.refs_0_
  2.0 1.2 reshape.103.refs_1_
  3.3 1.3 copy.22.refs_2_.refs_1_
  4.6 114.9 %forward.1 = (bf16[512,768]{1,0:T(8,128)(2,1)}, f32[2,768]{1,0:T(2,128)}, bf16[768,128]{1,0:T(8,128)(2,1)}, bf16[512,768]{1,0:T(8,128)(2,1)}, f32[512,1]{1,0:T(8...) custom-call(bf16[2,768]{1,0:T(2,128)(2,1)} %fusion.refs_0_, ...), custom_call_target="tpu_custom_call" | custom-call | tf_op jit(solution)/shard_map/forward/pallas_call | solution.py:766
  119.5 108.9 %backward.1 = (f32[576,128]{1,0:T(8,128)}, f32[576,128]{1,0:T(8,128)}, f32[144,128]{1,0:T(8,128)}, f32[432,128]{1,0:T(8,128)}, f32[144,128]{1,0:T(8,128)}, /*ind...) custom-call(bf16[512,768]{1,0:T(8,128)(2,1)} %bitcast.36, ...), custom_call_target="tpu_custom_call" | custom-call | tf_op jit(solution)/shard_map/backward/pallas_call | solution.py:1233
  228.4 3.8 %deliver.1 = (bf16[512,768]{1,0:T(8,128)(2,1)}, f32[512,768]{1,0:T(8,128)}, f32[432,128]{1,0:T(8,128)}, f32[144,128]{1,0:T(8,128)}, f32[432,128]{1,0:T(8,128)}, ...) custom-call(bf16[512,768]{1,0:T(8,128)(2,1)} %get-tuple-element.57.refs_0_, ...), custom_call_target="tpu_custom_call" | custom-call | tf_op jit(solution)/shard_map/deliver/pallas_call | solution.py:1274
  232.2 0.8 reshape.128
  233.0 0.7 dynamic_slice.3
  (1 shorter events, 0.0 us)
